TPU v7x, 512 devices: a whole 4x8x8 slice. The times are simulated.
512 devices in a mesh: seq: 64 (over x, y, core), head: 8 (over z).
Axes of the slice: x: 4, y: 8, z: 8, core: 2. Of those that a mesh axis runs over, the one named last changes fastest.
Arguments:
- tokens: float32 [8192, 2048], P('seq'), may hold values from -45 to 45
- cluster: int32 [8192, 1], P('seq'), may hold values from 0 to 255; in each aligned block of 128 rows (0 to 127, 128 to 255, ...) at most 4 rows name the same one
- w_query: float32 [2048, 1024], P('seq', 'head'), may hold values from -0.125 to 0.125
- w_key: float32 [2048, 1024], P('seq', 'head'), may hold values from -0.125 to 0.125
- w_value: float32 [2048, 1024], P('seq', 'head'), may hold values from -0.125 to 0.125
- grad_out: float32 [8192, 1024], P('seq', 'head'), may hold values from -6 to 6
Outputs:
- attended: float32 [8192, 1024], P('seq', 'head')
- grad_query: float32 [2048, 1024], P('seq', 'head')
- grad_key: float32 [2048, 1024], P('seq', 'head')
- grad_value: float32 [2048, 1024], P('seq', 'head')
Inputs may be any that keep to these rules, and one draw needn't show every extreme that they name: In the rows of one device (each aligned block of 128 rows), no cluster is named more than 4 times, a bound that some block reaches.
All inputs are finite; a program needn't handle non-finite values.
Results may differ from a plain program's by a relative error of at most 0.0003.
Values sent between devices are 32-bit elements; how exact they have to be, the bound alone decides.
A program may use at most 64 MiB of HBM per device.

v0:
```python
import math

import jax
import jax.numpy as jnp
from jax import lax
from jax.sharding import PartitionSpec as P

HS = 128
CLUST_DEV = 4
CAP = 4


highest = lax.Precision.HIGHEST


def probabilities(query, key_rows, occupied, head_count):
    groups, length, width = query.shape
    query_h = query.reshape(groups, length, head_count, width // head_count)
    key_h = key_rows.reshape(groups, length, head_count, width // head_count)
    score_scale = 1.0 / math.sqrt(width // head_count)
    scores = jnp.einsum("cihd,cjhd->chij", query_h, key_h, precision=highest) * score_scale
    positions = jnp.arange(length)
    causal = positions[None, :] <= positions[:, None]
    allowed = causal[None] & (occupied[:, None, :] > 0.5) | jnp.eye(length, dtype=bool)[None]
    allowed = allowed[:, None]
    row_max = jnp.max(jnp.where(allowed, scores, -1e30), axis=-1, keepdims=True)
    shifted = jnp.where(allowed, scores - row_max, -1e30)
    expos = jnp.exp(shifted)
    return expos / jnp.sum(expos, axis=-1, keepdims=True)


def attend(weights, value_rows, head_count):
    groups, length, width = value_rows.shape
    value_h = value_rows.reshape(groups, length, head_count, width // head_count)
    result = jnp.einsum("chij,cjhd->cihd", weights, value_h, precision=highest)
    return result.reshape(groups, length, width)


def backward(weights, query, key_rows, value_rows, cotangent, attended, head_count):
    groups, length, width = query.shape
    head_size = width // head_count
    score_scale = 1.0 / math.sqrt(head_size)
    query_h = query.reshape(groups, length, head_count, head_size)
    key_h = key_rows.reshape(groups, length, head_count, head_size)
    value_h = value_rows.reshape(groups, length, head_count, head_size)
    grad_h = cotangent.reshape(groups, length, head_count, head_size)
    out_h = attended.reshape(groups, length, head_count, head_size)
    grad_v = jnp.einsum("chij,cihd->cjhd", weights, grad_h, precision=highest)
    grad_prob = jnp.einsum("cihd,cjhd->chij", grad_h, value_h, precision=highest)
    row_term = jnp.einsum("cihd,cihd->chi", grad_h, out_h, precision=highest)[..., None]
    dscore = weights * (grad_prob - row_term)
    grad_q = jnp.einsum("chij,cjhd->cihd", dscore, key_h, precision=highest) * score_scale
    grad_k = jnp.einsum("chij,cihd->cjhd", dscore, query_h, precision=highest) * score_scale
    return (
        grad_q.reshape(groups, length, width),
        grad_k.reshape(groups, length, width),
        grad_v.reshape(groups, length, width),
    )


def local(tokens, cluster, w_query, w_key, w_value, grad_out):
    tok_rows = tokens.shape[0]
    width = w_query.shape[1]
    head_count = width // HS
    owners = lax.axis_size("seq")
    clusters = CLUST_DEV * owners
    pieces = (
        lax.all_gather(w_query, "seq", axis=0, tiled=True),
        lax.all_gather(w_key, "seq", axis=0, tiled=True),
        lax.all_gather(w_value, "seq", axis=0, tiled=True),
    )
    columns = tokens
    query, key_rows, value_rows = tuple(
        (
            jnp.dot(columns, piece, precision=highest, preferred_element_type=jnp.float32)
            for piece in pieces
        )
    )
    cluster_ids = cluster[:, 0]
    onehot = (cluster_ids[:, None] == jnp.arange(clusters, dtype=jnp.int32)[None, :]).astype(
        jnp.int32
    )
    strict = (jnp.arange(tok_rows)[:, None] > jnp.arange(tok_rows)[None, :]).astype(jnp.int32)
    before = jnp.dot(strict, onehot)
    rank_in = jnp.sum(onehot * before, axis=1)
    slot_index = cluster_ids * CAP + rank_in

    def to_slots(rows):
        buffer = jnp.zeros((clusters * CAP, width), jnp.float32).at[slot_index].set(rows)
        return buffer.reshape(clusters, CAP, width)

    def from_slots(buffer):
        return buffer.reshape(clusters * CAP, width)[slot_index]

    occupied = (
        jnp.zeros((clusters * CAP,), jnp.float32).at[slot_index].set(1.0).reshape(clusters, CAP)
    )
    owner_q, owner_k, owner_v, owner_occ = (
        lax.all_to_all(to_slots(query), "seq", split_axis=0, concat_axis=1, tiled=True),
        lax.all_to_all(to_slots(key_rows), "seq", split_axis=0, concat_axis=1, tiled=True),
        lax.all_to_all(to_slots(value_rows), "seq", split_axis=0, concat_axis=1, tiled=True),
        lax.all_to_all(occupied, "seq", split_axis=0, concat_axis=1, tiled=True),
    )
    weights = probabilities(owner_q, owner_k, owner_occ, head_count)
    owner_out = attend(weights, owner_v, head_count)
    attended = from_slots(lax.all_to_all(owner_out, "seq", split_axis=1, concat_axis=0, tiled=True))
    owner_grad = lax.all_to_all(to_slots(grad_out), "seq", split_axis=0, concat_axis=1, tiled=True)
    again = probabilities(owner_q, owner_k, owner_occ, head_count)
    grad_q, grad_k, grad_v = backward(
        again, owner_q, owner_k, owner_v, owner_grad, owner_out, head_count
    )
    back_q, back_k, back_v = (
        lax.all_to_all(grad_q, "seq", split_axis=1, concat_axis=0, tiled=True),
        lax.all_to_all(grad_k, "seq", split_axis=1, concat_axis=0, tiled=True),
        lax.all_to_all(grad_v, "seq", split_axis=1, concat_axis=0, tiled=True),
    )
    combined = jnp.concatenate([from_slots(back_q), from_slots(back_k), from_slots(back_v)], axis=1)
    columns = tokens
    shares = lax.psum_scatter(
        jnp.dot(columns.T, combined, precision=highest, preferred_element_type=jnp.float32),
        "seq",
        scatter_dimension=0,
        tiled=True,
    )
    return (attended, shares[:, :width], shares[:, width : 2 * width], shares[:, 2 * width :])


def solution(mesh):
    in_specs = (
        P("seq", None),
        P("seq", None),
        P("seq", "head"),
        P("seq", "head"),
        P("seq", "head"),
        P("seq", "head"),
    )
    out_specs = (P("seq", "head"), P("seq", "head"), P("seq", "head"), P("seq", "head"))
    return jax.shard_map(local, mesh=mesh, in_specs=in_specs, out_specs=out_specs, check_vma=False)
```

profile of v0, /device:TPU:6, one launch (start us, length us, event | category | flops | bytes accessed | tf_op | source)
XLA Modules:
  0.0 537.0 jit_solution(14906327756888436326)
XLA Ops:
  12.2 10.8 %all-to-all-start.1 = ((f32[64,4,4]{2,1,0:T(4,128)}), f32[64,4,4]{2,1,0:T(4,128)S(1)}, u32[]{:S(2)}, u32[]{:S(2)}) async-start(f32[64,4,4]{2,1,0:T(4,128)} %all_to_all.101), calls=%async_computation.1 | async-start | bytes 262144 | tf_op jit(solution)/shard_map/all_to_all | solution.py:102
  23.0 2.0 scatter_custom_fusion.4
  25.0 6.9 %all-to-all-done.1 = f32[64,4,4]{2,1,0:T(4,128)S(1)} async-done(((f32[64,4,4]{2,1,0:T(4,128)}), f32[64,4,4]{2,1,0:T(4,128)S(1)}, u32[]{:S(2)}, u32[]{:S(2)}) %all-to-all-start.1) | async-done | bytes 4128 | tf_op jit(solution)/shard_map/all_to_all | solution.py:102
  31.9 6.4 %all-to-all-start.5 = ((f32[256,4,128]{2,1,0:T(4,128)}), f32[256,4,128]{2,1,0:T(4,128)S(1)}, u32[]{:S(2)}, u32[]{:S(2)}) async-start(f32[256,4,128]{2,1,0:T(4,128)} %bitcast.22), calls=%async_computation.5 | async-start | bytes 1048576 | tf_op jit(solution)/shard_map/all_to_all | solution.py:107
  39.0 58.2 %all-gather.8.cloned.1.call-done = f32[2048,128]{1,0:T(8,128)} async-done(((f32[32,128]{1,0:T(8,128)}), f32[2048,128]{1,0:T(8,128)}) %all-gather.8.cloned.1.call-update) | async-done | bytes 1048592 | tf_op jit(solution)/shard_map/all_gather | solution.py:69
  97.3 2.4 fusion.40
  99.6 1.7 scatter_custom_fusion.3
  101.3 8.3 %all-to-all-start.3 = ((f32[256,4,128]{2,1,0:T(4,128)}), f32[256,4,128]{2,1,0:T(4,128)S(1)}, u32[]{:S(2)}, u32[]{:S(2)}) async-start(f32[256,4,128]{2,1,0:T(4,128)} %bitcast.12), calls=%async_computation.3 | async-start | bytes 1048576 | tf_op jit(solution)/shard_map/all_to_all | solution.py:100
  109.6 71.0 %all-gather.6.cloned.1.call-done = f32[2048,128]{1,0:T(8,128)} async-done(((f32[32,128]{1,0:T(8,128)}), f32[2048,128]{1,0:T(8,128)}) %all-gather.6.cloned.1.call-update) | async-done | bytes 1048592 | tf_op jit(solution)/shard_map/all_gather | solution.py:68
  180.6 2.4 fusion.39
  183.0 1.7 scatter_custom_fusion.2
  184.6 8.3 %all-to-all-start.2 = ((f32[256,4,128]{2,1,0:T(4,128)}), f32[256,4,128]{2,1,0:T(4,128)S(1)}, u32[]{:S(2)}, u32[]{:S(2)}) async-start(f32[256,4,128]{2,1,0:T(4,128)} %bitcast.8), calls=%async_computation.2 | async-start | bytes 1048576 | tf_op jit(solution)/shard_map/all_to_all | solution.py:99
  192.9 71.1 %all-gather.4.cloned.1.call-done = f32[2048,128]{1,0:T(8,128)} async-done(((f32[32,128]{1,0:T(8,128)}), f32[2048,128]{1,0:T(8,128)}) %all-gather.4.cloned.1.call-update) | async-done | bytes 1048592 | tf_op jit(solution)/shard_map/all_gather | solution.py:70
  264.0 2.4 fusion.38
  268.0 8.3 %all-to-all-start = ((f32[256,4,128]{2,1,0:T(4,128)}), f32[256,4,128]{2,1,0:T(4,128)S(1)}, u32[]{:S(2)}, u32[]{:S(2)}) async-start(f32[256,4,128]{2,1,0:T(4,128)} %bitcast.3), calls=%async_computation | async-start | bytes 1048576 | tf_op jit(solution)/shard_map/all_to_all | solution.py:101
  278.8 14.3 %all-to-all-done = f32[256,4,128]{2,1,0:T(4,128)S(1)} async-done(((f32[256,4,128]{2,1,0:T(4,128)}), f32[256,4,128]{2,1,0:T(4,128)S(1)}, u32[]{:S(2)}, u32[]{:S(2)}) %all-to-all-start) | async-done | bytes 524320 | tf_op jit(solution)/shard_map/all_to_all | solution.py:101
  295.1 1.9 multiply_reduce_fusion
  298.2 2.0 fusion.10
  300.2 2.1 copy.77
  302.3 7.1 %all-to-all-start.7 = ((f32[4,256,128]{2,0,1:T(4,128)}), f32[4,256,128]{2,0,1:T(4,128)}, u32[]{:S(2)}, u32[]{:S(2)}) async-start(f32[4,256,128]{2,0,1:T(4,128)} %copy.77), calls=%async_computation.7 | async-start | bytes 1048576 | tf_op jit(solution)/shard_map/all_to_all | solution.py:114
  309.4 1.9 fusion.11
  311.3 2.0 copy.72
  313.3 12.7 %all-to-all-done.7 = f32[4,256,128]{2,0,1:T(4,128)} async-done(((f32[4,256,128]{2,0,1:T(4,128)}), f32[4,256,128]{2,0,1:T(4,128)}, u32[]{:S(2)}, u32[]{:S(2)}) %all-to-all-start.7) | async-done | bytes 524320 | tf_op jit(solution)/shard_map/all_to_all | solution.py:114
  326.0 6.9 %all-to-all-start.6 = ((f32[4,256,128]{2,0,1:T(4,128)}), f32[4,256,128]{2,0,1:T(4,128)S(1)}, u32[]{:S(2)}, u32[]{:S(2)}) async-start(f32[4,256,128]{2,0,1:T(4,128)} %copy.72), calls=%async_computation.6 | async-start | bytes 1048576 | tf_op jit(solution)/shard_map/all_to_all | solution.py:113
  332.9 2.5 convolution_bitcast_fusion.1
  336.4 13.2 %all-to-all-done.6 = f32[4,256,128]{2,0,1:T(4,128)S(1)} async-done(((f32[4,256,128]{2,0,1:T(4,128)}), f32[4,256,128]{2,0,1:T(4,128)S(1)}, u32[]{:S(2)}, u32[]{:S(2)}) %all-to-all-start.6) | async-done | bytes 524320 | tf_op jit(solution)/shard_map/all_to_all | solution.py:113
  349.6 6.9 %all-to-all-start.8 = ((f32[4,256,128]{2,0,1:T(4,128)}), f32[4,256,128]{2,0,1:T(4,128)S(1)}, u32[]{:S(2)}, u32[]{:S(2)}) async-start(f32[4,256,128]{2,0,1:T(4,128)} %copy.82), calls=%async_computation.8 | async-start | bytes 1048576 | tf_op jit(solution)/shard_map/all_to_all | solution.py:115
  359.2 14.0 %all-to-all-done.8 = f32[4,256,128]{2,0,1:T(4,128)S(1)} async-done(((f32[4,256,128]{2,0,1:T(4,128)}), f32[4,256,128]{2,0,1:T(4,128)S(1)}, u32[]{:S(2)}, u32[]{:S(2)}) %all-to-all-start.8) | async-done | bytes 524320 | tf_op jit(solution)/shard_map/all_to_all | solution.py:115
  374.0 4.3 convolution_bitcast_fusion
  378.4 3.5 copy.101
  383.2 23.4 %all_to_all.133 = f32[4,256,128]{2,0,1:T(4,128)S(1)} all-to-all(f32[4,256,128]{2,0,1:T(4,128)S(1)} %copy.64), channel_id=1, replica_groups=mesh['seq'=64,'head'=8] {'seq'}, dimensions={1} | all-to-all | bytes 1048576 | tf_op jit(solution)/shard_map/all_to_all | solution.py:106
  407.9 121.2 %reduce-scatter.4.cloned.1.call-done = f32[32,384]{1,0:T(8,128)} async-done(((f32[2048,384]{1,0:T(8,128)}), f32[32,384]{1,0:T(8,128)}) %reduce-scatter.4.cloned.1.call-update) | async-done | bytes 49168
  (63 shorter events, 21.3 us)
Async XLA Ops:
  7.2 90.1 %copy-start = (f32[128,2048]{1,0:T(8,128)S(1)}, f32[128,2048]{1,0:T(8,128)}, u32[]{:S(2)}) copy-start(f32[128,2048]{1,0:T(8,128)} %param.6) | copy-start | bytes 3145732
  7.2 90.1 %all-gather.8.cloned.1.call-start = ((), (), s32[]{:S(2)}) async-start(), calls=%async_computation.12 | async-start | bytes 1064960 | tf_op jit(solution)/shard_map/all_gather | solution.py:69
  7.9 172.7 %all-gather.6.cloned.1.call-start = ((), (), s32[]{:S(2)}) async-start(), calls=%async_computation.11 | async-start | bytes 1064960 | tf_op jit(solution)/shard_map/all_gather | solution.py:68
  12.2 19.7 %all-to-all-start.1 = ((f32[64,4,4]{2,1,0:T(4,128)}), f32[64,4,4]{2,1,0:T(4,128)S(1)}, u32[]{:S(2)}, u32[]{:S(2)}) async-start(f32[64,4,4]{2,1,0:T(4,128)} %all_to_all.101), calls=%async_computation.1 | async-start | bytes 262144 | tf_op jit(solution)/shard_map/all_to_all | solution.py:102
  31.9 69.4 %all-to-all-start.5 = ((f32[256,4,128]{2,1,0:T(4,128)}), f32[256,4,128]{2,1,0:T(4,128)S(1)}, u32[]{:S(2)}, u32[]{:S(2)}) async-start(f32[256,4,128]{2,1,0:T(4,128)} %bitcast.22), calls=%async_computation.5 | async-start | bytes 1048576 | tf_op jit(solution)/shard_map/all_to_all | solution.py:107
  38.3 225.7 %all-gather.4.cloned.1.call-start = ((), (), s32[]{:S(2)}) async-start(), calls=%async_computation.10 | async-start | bytes 1064960 | tf_op jit(solution)/shard_map/all_gather | solution.py:70
  101.3 83.4 %all-to-all-start.3 = ((f32[256,4,128]{2,1,0:T(4,128)}), f32[256,4,128]{2,1,0:T(4,128)S(1)}, u32[]{:S(2)}, u32[]{:S(2)}) async-start(f32[256,4,128]{2,1,0:T(4,128)} %bitcast.12), calls=%async_computation.3 | async-start | bytes 1048576 | tf_op jit(solution)/shard_map/all_to_all | solution.py:100
  184.6 83.4 %all-to-all-start.2 = ((f32[256,4,128]{2,1,0:T(4,128)}), f32[256,4,128]{2,1,0:T(4,128)S(1)}, u32[]{:S(2)}, u32[]{:S(2)}) async-start(f32[256,4,128]{2,1,0:T(4,128)} %bitcast.8), calls=%async_computation.2 | async-start | bytes 1048576 | tf_op jit(solution)/shard_map/all_to_all | solution.py:99
  268.0 25.0 %all-to-all-start = ((f32[256,4,128]{2,1,0:T(4,128)}), f32[256,4,128]{2,1,0:T(4,128)S(1)}, u32[]{:S(2)}, u32[]{:S(2)}) async-start(f32[256,4,128]{2,1,0:T(4,128)} %bitcast.3), calls=%async_computation | async-start | bytes 1048576 | tf_op jit(solution)/shard_map/all_to_all | solution.py:101
  277.0 1.1 copy-start.1
  293.1 2.0 copy-start.5
  294.4 2.6 copy-start.2
  295.1 3.1 copy-start.6
  300.2 32.7 %copy-start.3 = (f32[4,64,4,128]{3,2,1,0:T(4,128)S(1)}, f32[4,64,4,128]{3,2,1,0:T(4,128)}, u32[]{:S(2)}) copy-start(f32[4,64,4,128]{3,2,1,0:T(4,128)} %copy-done.1) | copy-start | bytes 1572868
  302.3 23.7 %all-to-all-start.7 = ((f32[4,256,128]{2,0,1:T(4,128)}), f32[4,256,128]{2,0,1:T(4,128)}, u32[]{:S(2)}, u32[]{:S(2)}) async-start(f32[4,256,128]{2,0,1:T(4,128)} %copy.77), calls=%async_computation.7 | async-start | bytes 1048576 | tf_op jit(solution)/shard_map/all_to_all | solution.py:114
  326.0 23.6 %all-to-all-start.6 = ((f32[4,256,128]{2,0,1:T(4,128)}), f32[4,256,128]{2,0,1:T(4,128)S(1)}, u32[]{:S(2)}, u32[]{:S(2)}) async-start(f32[4,256,128]{2,0,1:T(4,128)} %copy.72), calls=%async_computation.6 | async-start | bytes 1048576 | tf_op jit(solution)/shard_map/all_to_all | solution.py:113
  349.6 23.6 %all-to-all-start.8 = ((f32[4,256,128]{2,0,1:T(4,128)}), f32[4,256,128]{2,0,1:T(4,128)S(1)}, u32[]{:S(2)}, u32[]{:S(2)}) async-start(f32[4,256,128]{2,0,1:T(4,128)} %copy.82), calls=%async_computation.8 | async-start | bytes 1048576 | tf_op jit(solution)/shard_map/all_to_all | solution.py:115
  356.6 172.6 %reduce-scatter.4.cloned.1.call-start = ((), (), s32[]{:S(2)}) async-start(), calls=%async_computation.13 | async-start | bytes 3194880
  381.9 1.0 copy-start.4
Sparse Core Ops, SparseCore 0:
  11.4 85.8 all-gather.7
  100.6 79.9 all-gather.5
  184.0 79.9 all-gather.3
  382.0 147.0 reduce-scatter.3
where the time goes:
time: 539 us; the launch traced here: 537 us
  waiting for transfers between devices  385 us (71%)
  starting transfers between devices  63 us (12%)
  local copies, waits for them, and re-layouts  27.4 us (5%)
  blocking collectives  23.4 us (4%)
  matrix products  22.9 us (4%)
  between operations  14.1 us (3%)
    unnamed x5, waiting for transfers between devices  123 us
    all_gather x1, waiting for transfers between devices, local(): lax.all_gather(w_value, 'seq', axis=0, tiled=True)  71.1 us
    all_gather x1, waiting for transfers between devices, local(): lax.all_gather(w_query, 'seq', axis=0, tiled=True)  71 us
    all_gather x1, waiting for transfers between devices, local(): lax.all_gather(w_key, 'seq', axis=0, tiled=True)  58.2 us
    all_to_all x1, blocking collectives, local(): lax.all_to_all(owner_out, 'seq', split_axis=1, concat_axis=0, tiled=True)  23.4 us
    all_to_all x1, waiting for transfers between devices, local(): lax.all_to_all(to_slots(value_rows), 'seq', split_axis=0, concat_axis=1,...  14.3 us
    all_to_all x1, waiting for transfers between devices, local(): lax.all_to_all(grad_v, 'seq', split_axis=1, concat_axis=0, tiled=True)  14 us
    all_to_all x1, waiting for transfers between devices, local(): lax.all_to_all(grad_q, 'seq', split_axis=1, concat_axis=0, tiled=True)  13.2 us
  transfers between devices with their start and end apart: 12, of which 9 were waited for; matrix products, arithmetic and copies ran while one was open for 6% of the time, Pallas kernels for 0%

commit v1 on v0

v1 whole, which is shorter than its diff:
```python
import functools
import math

import jax
import jax.numpy as jnp
from jax import lax
from jax.experimental import pallas as pl
from jax.experimental.pallas import tpu as pltpu
from jax.sharding import PartitionSpec as P

MESH = pl.DeviceIdType.MESH
F32 = jnp.float32
BF16 = jnp.bfloat16
X, Y, C = 4, 8, 2
T = 128
H = 128
D = 2048
SCALE = 1.0 / math.sqrt(H)
NEG = -1e30
COPIES = 256

NT = ((1,), (1,))
NN = ((1,), (0,))


def split(a):
    hi = a.astype(BF16)
    return hi, (a - hi.astype(F32)).astype(BF16)


def dot3(a, b, dims):
    def one(p, q):
        return lax.dot_general(p, q, (dims, ((), ())), preferred_element_type=F32)

    return one(a[0], b[0]) + (one(a[0], b[1]) + one(a[1], b[0]))


def kernel(
    tok_in, clu, wq, wk, wv, gout,
    att_o, grad_o,
    tok, wbuf, tokh, tokl, toth, totl, qb, gb, kv, cq, ck, ckb, pkb,
    kvh, kvl, kth, ktl, qgh, qgl, eb, gvb, ph, pl_, dh, dl, stb, al_s, rr_s,
    ob, obr, obl, gqb, gq_in, gq_half, gkv, gsib, gx, gw, gws, ga_r, ga_l, gbx, gb_r, gb_l, gax,
    send, recv, here,
):
    me = lax.axis_index("seq")
    c = lax.rem(me, C)
    y = lax.rem(me // C, Y)
    x = me // (C * Y)

    def yy(d):
        return lax.rem(y + (d + 2 * Y), Y)

    def xx(d):
        return lax.rem(x + (d + 2 * X), X)

    def dev(xd, yd, cd):
        return (xd * Y + yd) * C + cd

    right, left, sib = dev(x, yy(1), c), dev(x, yy(-1), c), dev(x, y, 1 - c)
    along = (1, right, 0), (-1, left, 1)
    copies = []

    def start(src, dst, device):
        i = len(copies)
        copy = pltpu.make_async_remote_copy(
            src_ref=src, dst_ref=dst, send_sem=send.at[i], recv_sem=recv.at[i],
            device_id={"seq": device}, device_id_type=MESH,
        )
        copy.start()
        copies.append(copy)
        return copy

    def share(ref, device):
        return start(ref, ref, device)

    near = [right, left, sib] + [dev(xx(d), y, c) for d in range(1, X)]
    barrier = pltpu.get_barrier_semaphore()
    for peer in near:
        pl.semaphore_signal(barrier, inc=1, device_id={"seq": peer}, device_id_type=MESH)

    local_copies = []

    def fetch(src, dst):
        copy = pltpu.make_async_copy(src, dst, here.at[len(local_copies)])
        copy.start()
        local_copies.append(copy)

    for half in range(2):
        for i, ref in enumerate((wq, wk, wv)):
            fetch(ref.at[pl.ds(half * 16, 16), :], wbuf.at[x, y, c, half, :, pl.ds(i * H, H)])
    fetch(gout, gb.at[y])
    fetch(tok_in, tok)
    ids = jnp.broadcast_to(clu[...].astype(F32), (8, T))
    cq[y] = ids
    ck[x, c] = ids
    for copy in local_copies[:6]:
        copy.wait()
    pl.semaphore_wait(barrier, len(near))

    class Gather:
        def __init__(self, slot, half):
            self.slot, self.half = slot, half
            self.sent = [[share(slot(y), to)] for _, to, _ in along]

        def step(self, k):
            for (sign, to, h), sent in zip(along, self.sent):
                sent[k - 1].wait_recv()
                if k < 4:
                    o = yy(-sign * k)
                    sent.append(share(self.slot(o) if k < 3 else self.half(o, h), to))

    class Scatter:
        def __init__(self, part, half, into, into_half):
            self.part, self.half, self.into, self.into_half = part, half, into, into_half
            self.sent = [[start(half(yy(4), h), into_half[h], to)] for _, to, h in along]

        def step(self, k):
            for (sign, to, h), sent in zip(along, self.sent):
                sent[k - 1].wait_recv()
                o = yy(sign * (4 - k))
                mine = self.part(o)
                if k == 1:
                    first = self.half(o, h)
                    first[...] += self.into_half[h][...]
                else:
                    mine[...] += self.into(h, k - 1)[...]
                if k < 4:
                    sent.append(start(mine, self.into(h, k), to))

    def arrived(k):
        return (yy(0),) if k == 0 else ((yy(4),) if k == 4 else (yy(-k), yy(k)))

    def ring_for(xo):
        return Gather(lambda o: wbuf.at[xo, o, c, 0], lambda o, h: wbuf.at[xo, o, c, 0, pl.ds(8 * h, 8)])

    a_x = {d: share(wbuf.at[x, y, c, 0], dev(xx(d), y, c)) for d in (1, 3, 2)}
    rings = [ring_for(x)]
    ring_b = Gather(lambda o: wbuf.at[x, o, c, 1], lambda o, h: wbuf.at[x, o, c, 1, pl.ds(8 * h, 8)])
    b_x = {}
    from_sib = []

    def spread(k):
        b_x[k] = [(o, [share(wbuf.at[x, o, c, 1], dev(xx(d), y, c)) for d in (1, 3, 2)]) for o in arrived(k)]

    def across(k):
        for o, landed in b_x[k]:
            for copy in landed:
                copy.wait_recv()
            from_sib.append(share(wbuf.at[:, o, c, 1], sib))

    spread(0)
    local_copies[7].wait()

    def halves(i, _):
        cols = pl.ds(pl.multiple_of(i * 128, 128), 128)
        block = tok[:, cols]
        hi, lo = split(block)
        tokh[:, cols] = hi
        tokl[:, cols] = lo
        hi, lo = split(jnp.transpose(block))
        toth[cols, :] = hi
        totl[cols, :] = lo
        return 0

    lax.fori_loop(0, 6, halves, 0)
    for d in (1, 3, 2):
        a_x[d].wait_recv()
        rings.append(ring_for(xx(-d)))
    from_sib.append(share(wbuf.at[:, y, c, 0], sib))
    local_copies[6].wait()
    for k in range(1, 5):
        rings[0].step(k)
        ring_b.step(k)
        spread(k)
        if k == 1:
            ring_g = Gather(lambda o: gb.at[o], lambda o, h: gb.at[o, pl.ds(64 * h, 64)])
        for ring in rings[1:]:
            ring.step(k)
        for o in arrived(k):
            from_sib.append(share(wbuf.at[:, o, c, 0], sib))
        if k > 1:
            ring_g.step(k - 1)
        across(k - 1)
        lax.fori_loop(3 + 3 * k, min(6 + 3 * k, D // 128), halves, 0)
    across(4)
    for copy in from_sib:
        copy.wait_recv()

    qkv = None
    for i in range(X):
        w = split(wbuf[i].reshape(D // X, 3 * H))
        cols = slice(i * (D // X), (i + 1) * (D // X))
        term = dot3((tokh[:, cols], tokl[:, cols]), w, NN)
        qkv = term if qkv is None else qkv + term
    qb[y] = qkv[:, 0:H]
    kv[0, x, c] = qkv[:, H:2 * H]
    kv[1, x, c] = qkv[:, 2 * H:]

    kv_x = {d: share(kv.at[:, x, c], dev(xx(d), y, c)) for d in (2, 1, 3)}
    kv_s = [share(kv.at[:, x, c], sib)]
    two = [share(qb.at[y], dev(x, yy(2 * sign), c)) for sign, _, _ in along]
    q_in = [share(qb.at[y], to) for _, to, _ in along]
    ids_in = [share(ck.at[x, c], dev(xx(d), y, c)) for d in range(1, X)]
    ids_in += [share(ck.at[x, c], dev(xx(d), y, 1 - c)) for d in range(X)]
    ids_in += [share(cq.at[y], dev(x, yy(d), c)) for d in range(1, Y)]

    def sides(xo, co):
        rows = pl.ds(pl.multiple_of((xo * C + co) * T, T), T)
        for n in range(2):
            block = kv[n, xo, co]
            hi, lo = split(block)
            kvh[n, rows, :] = hi
            kvl[n, rows, :] = lo
            hi, lo = split(jnp.transpose(block))
            kth[n, :, rows] = hi
            ktl[n, :, rows] = lo

    sides(x, c)
    kv_s[0].wait_recv()
    sides(x, 1 - c)
    for (sign, to, h), copy in zip(along, two):
        copy.wait_recv()
        o = yy(-2 * sign)
        q_in.append(share(qb.at[o, pl.ds(64 * h, 64)], dev(x, yy(2 * sign), c)))
        q_in.append(share(qb.at[o], to))
    ring_g.step(4)
    for copy in ids_in:
        copy.wait_recv()

    def keys(i, _):
        xo, co = i // C, lax.rem(i, C)
        ckb[i] = jnp.transpose(jnp.broadcast_to(ck[xo, co][0:1, :], (T, T)))
        pkb[i] = dev(xo, y, co) * T + lax.broadcasted_iota(jnp.int32, (T, T), 0)
        return 0

    lax.fori_loop(0, X * C, keys, 0)
    for d in (1, 3, 2):
        kv_x[d].wait_recv()
        kv_s.append(share(kv.at[:, xx(-d), c], sib))
        sides(xx(-d), c)
    for d, copy in zip((1, 3, 2), kv_s[1:]):
        copy.wait_recv()
        sides(xx(-d), 1 - c)
    for copy in q_in:
        copy.wait_recv()

    KEYS = X * C * T

    def forward(i, _):
        q = split(qb[pl.ds(2 * i, 2)].reshape(2 * T, H))
        g = split(gb[pl.ds(2 * i, 2)].reshape(2 * T, H))
        qgh[0, i], qgl[0, i] = q
        qgh[1, i], qgl[1, i] = g
        s = dot3((kvh[0], kvl[0]), q, NT) * SCALE
        gv = dot3((kvh[1], kvl[1]), g, NT)
        for n in range(2):
            o = 2 * i + n
            lanes = slice(n * T, (n + 1) * T)
            position = dev(x, o, c) * T + lax.broadcasted_iota(jnp.int32, (1, T), 1)
            same = ckb[...].reshape(KEYS, T) == cq[o][0:1, :]
            allowed = same & (pkb[...].reshape(KEYS, T) <= position)
            masked = jnp.where(allowed, s[:, lanes], NEG)
            top = jnp.max(masked, axis=0, keepdims=True)
            e = jnp.where(allowed, jnp.exp(masked - top), 0.0)
            gvn = gv[:, lanes]
            eb[o] = e
            gvb[o] = gvn
            stb[y, 0, pl.ds(o, 1), :] = top
            stb[y, 1, pl.ds(o, 1), :] = jnp.sum(e, axis=0, keepdims=True)
            stb[y, 2, pl.ds(o, 1), :] = jnp.sum(e * gvn, axis=0, keepdims=True)
        return 0

    lax.fori_loop(0, Y // 2, forward, 0)

    stats = [share(stb.at[y], dev(x, yy(d), c)) for d in (4, 3, 5, 2, 6, 1, 7)]
    for copy in stats:
        copy.wait_recv()
    top = stb[0, 0]
    for o in range(1, Y):
        top = jnp.maximum(top, stb[o, 0])
    total = jnp.zeros_like(top)
    row = jnp.zeros_like(top)
    for o in range(Y):
        factor = jnp.exp(stb[o, 0] - top)
        total = total + stb[o, 1] * factor
        row = row + stb[o, 2] * factor
    al_s[...] = jnp.exp(stb[y, 0] - top) / total
    rr_s[...] = row / total

    def softmax(i, _):
        for n in range(2):
            o = 2 * i + n
            lanes = slice(n * T, (n + 1) * T)
            p = eb[o] * al_s[pl.ds(o, 1), :]
            ph[i, :, lanes], pl_[i, :, lanes] = split(p)
            dh[i, :, lanes], dl[i, :, lanes] = split(p * ((gvb[o] - rr_s[pl.ds(o, 1), :]) * SCALE))
        return 0

    lax.fori_loop(0, Y // 2, softmax, 0)

    def key_side(xo):
        rows = pl.ds(pl.multiple_of(xo * (C * T), C * T), C * T)
        for n, (hi, lo) in enumerate(((dh, dl), (ph, pl_))):
            def add(i, acc):
                return acc + dot3((hi[i, rows, :], lo[i, rows, :]), (qgh[n, i], qgl[n, i]), NN)

            acc = lax.fori_loop(0, Y // 2, add, jnp.zeros((C * T, H), F32))
            gkv[n, xo] = acc.reshape(C, T, H)
        return start(gkv.at[:, xo, 1 - c], gsib.at[:, xo], sib)

    def query_side(n, hi, lo, into):
        def body(i, _):
            r = dot3((kth[n], ktl[n]), (hi[i], lo[i]), NN)
            into[2 * i] = r[:, 0:T]
            into[2 * i + 1] = r[:, T:]
            return 0

        lax.fori_loop(0, Y // 2, body, 0)

    sib_in = {2: key_side(xx(2))}
    query_side(0, dh, dl, gqb)
    gq_4 = [start(gqb.at[yy(4), pl.ds(64 * h, 64)], gq_half.at[h], dev(x, yy(2 * sign), c)) for sign, _, h in along]
    gq_3 = [start(gqb.at[yy(3 * sign)], gq_in.at[h, 0], to) for sign, to, h in along]
    gq_1 = [start(gqb.at[yy(sign)], gq_in.at[h, 1], to) for sign, to, h in along]
    x_in = []

    def key_send(d):
        sib_in[d].wait_recv()
        gkv[:, xx(d), c] += gsib[:, xx(d)]
        if d:
            x_in.append(start(gkv.at[:, xx(d), c], gx.at[d - 1], dev(xx(d), y, c)))

    for d, last in ((1, 2), (3, 1), (0, 3)):
        sib_in[d] = key_side(xx(d))
        key_send(last)
    gq_2 = []
    for (sign, to, h), far, near_ in zip(along, gq_4, gq_3):
        o = yy(2 * sign)
        far.wait_recv()
        gqb[o, 64 * h:64 * h + 64, :] += gq_half[h]
        near_.wait_recv()
        gqb[o] += gq_in[h, 0]
        gq_2.append(start(gqb.at[o], gq_in.at[h, 2], dev(x, yy(2 * sign), c)))
    query_side(1, ph, pl_, ob)
    ring_o = Scatter(
        lambda o: ob.at[o], lambda o, h: ob.at[o, pl.ds(64 * h, 64)],
        lambda h, k: (obr, obl)[h].at[k], (obr.at[0, pl.ds(0, 64)], obl.at[0, pl.ds(64, 64)]),
    )
    key_send(0)
    for copy in gq_1 + gq_2 + x_in:
        copy.wait_recv()
    gq = (gqb[y] + (gq_in[0, 1] + gq_in[1, 1])) + (gq_in[0, 2] + gq_in[1, 2])
    parts = [jnp.transpose(gq)]
    for n in range(2):
        parts.append((gkv[n, x, c] + gx[0, n]) + (gx[1, n] + gx[2, n]))
    grads = split(jnp.concatenate(parts, axis=1))

    far_first = (2, 1, 3, 0)
    y_order = (4, 3, -3, 2, -2, 1, -1, 0)

    def project(d):
        xo = xx(d)
        rows = pl.ds(pl.multiple_of(xo * (D // X), D // X), D // X)
        gw[xo] = dot3((toth[rows, :], totl[rows, :]), grads, NN).reshape(Y, C, 2, 16, 3 * H)
        return start(gw.at[xo, :, 1 - c], gws.at[xo], sib)

    def sum_ring(d):
        xo = xx(d)
        return Scatter(
            lambda o: gw.at[xo, o, c, 0], lambda o, h: gw.at[xo, o, c, 0, pl.ds(8 * h, 8)],
            lambda h, k: (ga_r, ga_l)[h].at[d, k], (ga_r.at[d, 0, pl.ds(0, 8)], ga_l.at[d, 0, pl.ds(8, 8)]),
        )

    sums = {}
    bx_in = {}

    def launch(d, copy):
        copy.wait_recv()
        xo = xx(d)
        gw[xo, :, c] += gws[xo]
        sums[d] = sum_ring(d)
        if d:
            for n in y_order:
                o = yy(n)
                bx_in[d, n] = start(gw.at[xo, o, c, 1], gbx.at[d - 1, o], dev(xo, y, c))

    last = None
    for d in far_first:
        copy = project(d)
        if last is not None:
            launch(*last)
        last = (d, copy)
    launch(*last)

    def gathered(*numbers):
        for n in numbers:
            o = yy(n)
            for d in range(1, X):
                bx_in[d, n].wait_recv()
            gw[x, o, c, 1] += (gbx[0, o] + gbx[1, o]) + gbx[2, o]

    sums[2].step(1)
    gathered(4)
    ring_b = Scatter(
        lambda o: gw.at[x, o, c, 1], lambda o, h: gw.at[x, o, c, 1, pl.ds(8 * h, 8)],
        lambda h, k: (gb_r, gb_l)[h].at[k], (gb_r.at[0, pl.ds(0, 8)], gb_l.at[0, pl.ds(8, 8)]),
    )
    a_in = []
    for k in range(1, 5):
        for d in far_first:
            if (d, k) != (2, 1):
                sums[d].step(k)
            if k == 4 and d:
                a_in.append(start(gw.at[xx(d), y, c, 0], gax.at[d - 1], dev(xx(d), y, c)))
        gathered(*((4 - k, k - 4) if k < 4 else (0,)))
        ring_b.step(k)
        ring_o.step(k)
    att_o[...] = jnp.transpose(ob[y])
    grad_o[16:32, :] = gw[x, y, c, 1]
    for copy in a_in:
        copy.wait_recv()
    grad_o[0:16, :] = (gw[x, y, c, 0] + gax[0]) + (gax[1] + gax[2])
    for copy in copies:
        copy.wait_send()


def results(att, grad, att_o, gq_o, gk_o, gv_o):
    att_o[...] = att[...]
    for i, ref in enumerate((gq_o, gk_o, gv_o)):
        ref[...] = grad[:, i * H:(i + 1) * H]


def local(tokens, cluster, w_query, w_key, w_value, grad_out):
    vmem = pl.BlockSpec(memory_space=pltpu.VMEM)
    hbm = pl.BlockSpec(memory_space=pl.ANY)
    W3 = 3 * H
    keys = X * C * T
    pairs = Y // 2
    scratch = [
        pltpu.VMEM((T, D), F32),
        pltpu.VMEM((X, Y, C, 2, 16, W3), F32),
        pltpu.VMEM((T, D), BF16), pltpu.VMEM((T, D), BF16),
        pltpu.VMEM((D, T), BF16), pltpu.VMEM((D, T), BF16),
        pltpu.VMEM((Y, T, H), F32), pltpu.VMEM((Y, T, H), F32),
        pltpu.VMEM((2, X, C, T, H), F32),
        pltpu.VMEM((Y, 8, T), F32), pltpu.VMEM((X, C, 8, T), F32),
        pltpu.VMEM((X * C, T, T), F32), pltpu.VMEM((X * C, T, T), jnp.int32),
        pltpu.VMEM((2, keys, H), BF16), pltpu.VMEM((2, keys, H), BF16),
        pltpu.VMEM((2, H, keys), BF16), pltpu.VMEM((2, H, keys), BF16),
        pltpu.VMEM((2, pairs, 2 * T, H), BF16), pltpu.VMEM((2, pairs, 2 * T, H), BF16),
        pltpu.VMEM((Y, keys, T), F32), pltpu.VMEM((Y, keys, T), F32),
        pltpu.VMEM((pairs, keys, 2 * T), BF16), pltpu.VMEM((pairs, keys, 2 * T), BF16),
        pltpu.VMEM((pairs, keys, 2 * T), BF16), pltpu.VMEM((pairs, keys, 2 * T), BF16),
        pltpu.VMEM((Y, 3, Y, T), F32),
        pltpu.VMEM((Y, T), F32), pltpu.VMEM((Y, T), F32),
        pltpu.VMEM((Y, H, T), F32),
        pltpu.VMEM((4, H, T), F32), pltpu.VMEM((4, H, T), F32),
        pltpu.VMEM((Y, H, T), F32),
        pltpu.VMEM((2, 3, H, T), F32), pltpu.VMEM((2, H // 2, T), F32),
        pltpu.VMEM((2, X, C, T, H), F32),
        pltpu.VMEM((2, X, T, H), F32),
        pltpu.VMEM((X - 1, 2, T, H), F32),
        pltpu.VMEM((X, Y, C, 2, 16, W3), F32),
        pltpu.VMEM((X, Y, 2, 16, W3), F32),
        pltpu.VMEM((X, 4, 16, W3), F32), pltpu.VMEM((X, 4, 16, W3), F32),
        pltpu.VMEM((X - 1, Y, 16, W3), F32),
        pltpu.VMEM((4, 16, W3), F32), pltpu.VMEM((4, 16, W3), F32),
        pltpu.VMEM((X - 1, 16, W3), F32),
        pltpu.SemaphoreType.DMA((COPIES,)),
        pltpu.SemaphoreType.DMA((COPIES,)),
        pltpu.SemaphoreType.DMA((8,)),
    ]
    att, grad = pl.pallas_call(
        kernel,
        out_shape=(
            jax.ShapeDtypeStruct((T, H), F32),
            jax.ShapeDtypeStruct((D // 64, W3), F32),
        ),
        in_specs=[hbm, vmem, hbm, hbm, hbm, hbm],
        out_specs=(vmem,) * 2,
        scratch_shapes=scratch,
        compiler_params=pltpu.CompilerParams(
            collective_id=0, has_side_effects=True, vmem_limit_bytes=58 * 1024 * 1024
        ),
        name="routing",
    )(tokens, cluster.reshape(1, T), w_query, w_key, w_value, grad_out)
    part = jax.ShapeDtypeStruct((D // 64, H), F32)
    return pl.pallas_call(
        results,
        out_shape=(jax.ShapeDtypeStruct((T, H), F32), part, part, part),
        in_specs=[vmem] * 2,
        out_specs=(vmem,) * 4,
        name="results",
    )(att, grad)


def solution(mesh):
    in_specs = (P("seq", None), P("seq", None)) + (P("seq", "head"),) * 4
    out_specs = (P("seq", "head"),) * 4
    return jax.shard_map(local, mesh=mesh, in_specs=in_specs, out_specs=out_specs, check_vma=False)
```

time: 539 us -> 104 us (0.19)
  waiting for transfers between devices: 385 us -> 0 us
  Pallas kernels: 0 us -> 103 us
  starting transfers between devices: 63 us -> 0 us
  local copies, waits for them, and re-layouts: 27.4 us -> 0 us
  blocking collectives: 23.4 us -> 0 us
  matrix products: 22.9 us -> 0 us
  between operations: 14.1 us -> 0.64 us
    all_gather x3 -> x0, waiting for transfers between devices: 200 us -> none  [the longest x1 71.1 us: local(): lax.all_gather(w_value, 'seq', axis=0, tiled=True)]
    unnamed x5 -> x0, waiting for transfers between devices: 123 us -> none
    pallas_call x0 -> x2, Pallas kernels: none -> 103 us  [the longest x1 101 us: local(): pl.pallas_call(kernel, out_shape=(jax.ShapeDtypeStruct((T, H), F32), jax....]
    all_to_all x8 -> x0, starting transfers between devices: 62.9 us -> none  [the longest x1 10.8 us: local(): lax.all_to_all(occupied, 'seq', split_axis=0, concat_axis=1, tiled=True)]
    all_to_all x8 -> x0, waiting for transfers between devices: 61.1 us -> none  [the longest x1 14.3 us: local(): lax.all_to_all(to_slots(value_rows), 'seq', split_axis=0, concat_axis=1,...]
    all_to_all x1 -> x0, blocking collectives: 23.4 us -> none  [local(): lax.all_to_all(owner_out, 'seq', split_axis=1, concat_axis=0, tiled=True)]
    dot_general x11 -> x0, matrix products: 22.9 us -> none  [the longest x3 7.08 us: local(): jnp.dot(columns, piece, precision=highest, preferred_element_type=jnp.flo...]
    scatter x5 -> x0, local copies, waits for them, and re-layouts: 7.92 us -> none  [the longest x4 6.94 us: to_slots(): jnp.zeros((clusters * CAP, width), jnp.float32).at[slot_index].set(rows)]
  transfers between devices with their start and end apart: 12 -> 0, of which waited for: 9 -> 0; matrix products, arithmetic and copies ran while one was open for 6% -> 0% of each run, Pallas kernels for 0% -> 0%
where the time goes in v1:
time: 104 us; the launch traced here: 103 us
  Pallas kernels  103 us (99%)
    pallas_call x1, Pallas kernels, local(): pl.pallas_call(kernel, out_shape=(jax.ShapeDtypeStruct((T, H), F32), jax....  101 us

profile of v1, /device:TPU:6, one launch (start us, length us, event | category | flops | bytes accessed | tf_op | source)
XLA Modules:
  0.0 103.2 jit_solution(1680194718433963639)
XLA Ops:
  0.6 101.0 %routing.1 = (f32[128,128]{1,0:T(8,128)}, f32[32,384]{1,0:T(8,128)}) custom-call(f32[128,2048]{1,0:T(8,128)} %tok_in.1, s32[1,128]{1,0:T(1,128)} %bitcast.1, f32[32,128]{1,0:T(8,128)} %wq.1, f32[32,128]{1,0:T(8,128)} %wk.1, f32[32,128]{1,0:T(8,128)} %wv.1, f32[128,128]{1,0:T(8,128)} %gout.1), custom_call_target="tpu_custom_call" | custom-call | tf_op jit(solution)/shard_map/routing/pallas_call | solution.py:474
  101.7 1.5 %results.1 = (f32[128,128]{1,0:T(8,128)}, f32[32,128]{1,0:T(8,128)}, f32[32,128]{1,0:T(8,128)}, f32[32,128]{1,0:T(8,128)}) custom-call(f32[128,128]{1,0:T(8,128)} %get-tuple-element.6.att, f32[32,384]{1,0:T(8,128)} %get-tuple-element.7.grad), custom_call_target="tpu_custom_call" | custom-call | tf_op jit(solution)/shard_map/results/pallas_call | solution.py:489

commit v2 on v1

v2 whole, which is shorter than its diff:
```python
import functools
import math

import jax
import jax.numpy as jnp
from jax import lax
from jax.experimental import pallas as pl
from jax.experimental.pallas import tpu as pltpu
from jax.sharding import PartitionSpec as P

MESH = pl.DeviceIdType.MESH
F32 = jnp.float32
BF16 = jnp.bfloat16
X, Y, C = 4, 8, 2
T = 128
H = 128
D = 2048
SCALE = 1.0 / math.sqrt(H)
NEG = -1e30
COPIES = 136
ROWS = 8192

NT = ((1,), (1,))
NN = ((1,), (0,))


def split(a):
    hi = a.astype(BF16)
    return hi, (a - hi.astype(F32)).astype(BF16)


def dot3(a, b, dims):
    def one(p, q):
        return lax.dot_general(p, q, (dims, ((), ())), preferred_element_type=F32)

    return one(a[0], b[0]) + (one(a[0], b[1]) + one(a[1], b[0]))


def kernel(
    tok_in, clu, wq, wk, wv, gout,
    att_o, grad_o,
    tok, wbuf, tokh, tokl, toth, totl, qb, gb, kv, cq, ck, ckb, pkb,
    kvc, kvt, qsc, gsc, eb, gvb, eh, el, dh, dl, mlb, rb, al_s, rr_s,
    ob, obr, obl, gqb, gq_in, gq_half, gkv, gsib, gx, gw, gws, ga_r, ga_l, gbx, gb_r, gb_l, gax,
    sizer, send, recv, here,
):
    me = lax.axis_index("seq")
    c = lax.rem(me, C)
    y = lax.rem(me // C, Y)
    x = me // (C * Y)

    def yy(d):
        return lax.rem(y + (d + 2 * Y), Y)

    def xx(d):
        return lax.rem(x + (d + 2 * X), X)

    def dev(xd, yd, cd):
        return (xd * Y + yd) * C + cd

    right, left, sib = dev(x, yy(1), c), dev(x, yy(-1), c), dev(x, y, 1 - c)
    along = (1, right, 0), (-1, left, 1)
    groups = []
    sends = [0]

    class Batch:
        def __init__(self):
            self.rows, self.i = 0, len(groups)
            groups.append(self)

        def start(self, src, dst, device):
            rows = math.prod(src.shape) // 128
            if sends[-1] + rows > ROWS:
                sends.append(0)
            pltpu.make_async_remote_copy(
                src_ref=src, dst_ref=dst, send_sem=send.at[len(sends) - 1], recv_sem=recv.at[self.i],
                device_id={"seq": device}, device_id_type=MESH,
            ).start()
            sends[-1] += rows
            self.rows += rows
            return self

        def share(self, ref, device):
            return self.start(ref, ref, device)

        def wait_recv(self):
            some = sizer.at[pl.ds(0, self.rows)]
            pltpu.make_async_copy(some, some, recv.at[self.i]).wait()

    def start(src, dst, device):
        return Batch().start(src, dst, device)

    def share(ref, device):
        return Batch().share(ref, device)

    near = [dev(x, yy(d), c) for d in (1, -1, 2, -2)] + [dev(xx(d), y, c) for d in range(1, X)] + [sib]
    barrier = pltpu.get_barrier_semaphore()
    for peer in near:
        pl.semaphore_signal(barrier, inc=1, device_id={"seq": peer}, device_id_type=MESH)

    local_copies = []

    def fetch(src, dst):
        copy = pltpu.make_async_copy(src, dst, here.at[len(local_copies)])
        copy.start()
        local_copies.append(copy)

    for half in range(2):
        for i, ref in enumerate((wq, wk, wv)):
            fetch(ref.at[pl.ds(half * 16, 16), :], wbuf.at[x, y, c, half, :, pl.ds(i * H, H)])
    fetch(gout, gb.at[y])
    fetch(tok_in, tok)
    ids = jnp.broadcast_to(clu[...].astype(F32), (8, T))
    cq[y] = ids
    ck[x, c] = ids
    for copy in local_copies[:6]:
        copy.wait()
    pl.semaphore_wait(barrier, len(near))

    class Gather:
        def __init__(self, slots, halves):
            self.slots, self.halves = slots, halves
            self.two = [self.share(slots(y), dev(x, yy(2 * sign), c)) for sign, _, _ in along]
            self.one = [self.share(slots(y), to) for _, to, _ in along]

        def share(self, refs, device):
            batch = Batch()
            for ref in refs:
                batch.share(ref, device)
            return batch

        def step(self):
            self.far = []
            for (sign, to, h), copy in zip(along, self.two):
                copy.wait_recv()
                o = yy(-2 * sign)
                self.far.append(self.share(self.halves(o, h), dev(x, yy(2 * sign), c)))
                self.far.append(self.share(self.slots(o), to))
            for copy in self.one:
                copy.wait_recv()

        def finish(self):
            for copy in self.far:
                copy.wait_recv()

    class Sum:
        def __init__(self, parts, halves, into, into_half):
            self.parts, self.halves, self.into, self.into_half = parts, halves, into, into_half
            self.four = [
                self.start(halves(yy(4), h), into_half(h), dev(x, yy(2 * sign), c)) for sign, _, h in along
            ]
            self.three = [self.start(parts(yy(3 * sign)), into(h, 0), to) for sign, to, h in along]

        def start(self, src, dst, device):
            batch = Batch()
            for a, b in zip(src, dst):
                batch.start(a, b, device)
            return batch

        def step(self):
            self.two = []
            for (sign, _, h), four, three in zip(along, self.four, self.three):
                o = yy(2 * sign)
                four.wait_recv()
                for a, b in zip(self.halves(o, h), self.into_half(h)):
                    a[...] += b[...]
                three.wait_recv()
                for a, b in zip(self.parts(o), self.into(h, 0)):
                    a[...] += b[...]
                self.two.append(self.start(self.parts(o), self.into(h, 2), dev(x, yy(2 * sign), c)))

        def near(self):
            self.one = [self.start(self.parts(yy(sign)), self.into(h, 1), to) for sign, to, h in along]

        def finish(self):
            for copy in self.one + self.two:
                copy.wait_recv()
            for k in (1, 2):
                for h in (0, 1):
                    for a, b in zip(self.parts(y), self.into(h, k)):
                        a[...] += b[...]

    class Scatter:
        def __init__(self, part, half, into, into_half):
            self.part, self.half, self.into, self.into_half = part, half, into, into_half
            self.sent = [[start(half(yy(4), h), into_half[h], to)] for _, to, h in along]

        def step(self, k):
            for (sign, to, h), sent in zip(along, self.sent):
                sent[k - 1].wait_recv()
                o = yy(sign * (4 - k))
                mine = self.part(o)
                if k == 1:
                    first = self.half(o, h)
                    first[...] += self.into_half[h][...]
                else:
                    mine[...] += self.into(h, k - 1)[...]
                if k < 4:
                    sent.append(start(mine, self.into(h, k), to))

    def tree_for(*xs):
        return Gather(
            lambda o: [wbuf.at[i, o, c, 0] for i in xs],
            lambda o, h: [wbuf.at[i, o, c, 0, pl.ds(8 * h, 8)] for i in xs],
        )

    a_x = Batch()
    for d in (1, 3, 2):
        a_x.share(wbuf.at[x, y, c, 0], dev(xx(d), y, c))
    tree_own = tree_for(x)
    tree_b = Gather(lambda o: [wbuf.at[x, o, c, 1]], lambda o, h: [wbuf.at[x, o, c, 1, pl.ds(8 * h, 8)]])
    b_x = []
    sib_a, sib_b = Batch(), Batch()

    def spread(*numbers):
        for n in numbers:
            o, batch = yy(n), Batch()
            for d in (1, 3, 2):
                batch.share(wbuf.at[x, o, c, 1], dev(xx(d), y, c))
            b_x.append((o, batch))

    def across(count):
        for o, batch in b_x[:count]:
            batch.wait_recv()
            sib_b.share(wbuf.at[:, o, c, 1], sib)
        del b_x[:count]

    def over(*numbers):
        for n in numbers:
            sib_a.share(wbuf.at[:, yy(n), c, 0], sib)

    spread(0)
    local_copies[7].wait()

    def halves(i, _):
        cols = pl.ds(pl.multiple_of(i * 128, 128), 128)
        block = tok[:, cols]
        hi, lo = split(block)
        tokh[:, cols] = hi
        tokl[:, cols] = lo
        hi, lo = split(jnp.transpose(block))
        toth[cols, :] = hi
        totl[cols, :] = lo
        return 0

    lax.fori_loop(0, 8, halves, 0)
    local_copies[6].wait()
    a_x.wait_recv()
    tree_rest = tree_for(*[xx(d) for d in range(1, X)])
    over(0)
    tree_own.step()
    tree_b.step()
    spread(2, -2, 1, -1)
    lax.fori_loop(8, 12, halves, 0)
    across(1)
    tree_own.finish()
    tree_b.finish()
    spread(3, -3, 4)
    tree_rest.step()
    tree_g = Gather(lambda o: [gb.at[o]], lambda o, h: [gb.at[o, pl.ds(64 * h, 64)]])
    over(1, -1, 2, -2)
    across(4)
    lax.fori_loop(12, D // 128, halves, 0)
    tree_rest.finish()
    over(3, -3, 4)
    across(3)
    sib_a.wait_recv()
    sib_b.wait_recv()

    qkv = None
    for i in range(X):
        w = split(wbuf[i].reshape(D // X, 3 * H))
        cols = slice(i * (D // X), (i + 1) * (D // X))
        term = dot3((tokh[:, cols], tokl[:, cols]), w, NN)
        qkv = term if qkv is None else qkv + term
    qb[y] = qkv[:, 0:H]
    kv[0, x, c] = qkv[:, H:2 * H]
    kv[1, x, c] = qkv[:, 2 * H:]

    def spread_keys(n):
        across_x = {d: share(kv.at[n, x, c], dev(xx(d), y, c)) for d in (2, 1, 3)}
        return across_x, share(kv.at[n, x, c], sib)

    k_x, k_own = spread_keys(0)
    tree_q = Gather(lambda o: [qb.at[o]], lambda o, h: [qb.at[o, pl.ds(64 * h, 64)]])
    ids_in = Batch()
    for d in range(X):
        if d:
            ids_in.share(ck.at[x, c], dev(xx(d), y, c))
        ids_in.share(ck.at[x, c], dev(xx(d), y, 1 - c))
    for d in range(1, Y):
        ids_in.share(cq.at[y], dev(x, yy(d), c))
    v_x, v_own = spread_keys(1)

    def sides(n, xo, co):
        rows = pl.ds(pl.multiple_of((xo * C + co) * T, T), T)
        block = kv[n, xo, co]
        kvc[n, rows, 0:H], kvc[n, rows, H:] = split(block)
        kvt[n, 0:H, rows], kvt[n, H:, rows] = split(jnp.transpose(block))

    sides(0, x, c)
    sides(1, x, c)
    k_own.wait_recv()
    sides(0, x, 1 - c)
    tree_g.step()
    tree_q.step()
    ids_in.wait_recv()

    def keys(i, _):
        xo, co = i // C, lax.rem(i, C)
        ckb[i] = jnp.transpose(jnp.broadcast_to(ck[xo, co][0:1, :], (T, T)))
        pkb[i] = dev(xo, y, co) * T + lax.broadcasted_iota(jnp.int32, (T, T), 0)
        return 0

    lax.fori_loop(0, X * C, keys, 0)

    def collect(n, across_x):
        over = []
        for d in (1, 3, 2):
            across_x[d].wait_recv()
            over.append((d, share(kv.at[n, xx(-d), c], sib)))
            sides(n, xx(-d), c)
        return over

    k_sib = collect(0, k_x)
    for d, copy in k_sib:
        copy.wait_recv()
        sides(0, xx(-d), 1 - c)
    tree_q.finish()

    KEYS = X * C * T

    def against(n, rows):
        hi, lo = split(rows)
        both = lax.dot_general(kvc[n], jnp.concatenate([hi, hi], axis=1), (NT, ((), ())), preferred_element_type=F32)
        return both + lax.dot_general(kvc[n, :, 0:H], lo, (NT, ((), ())), preferred_element_type=F32)

    def scores(i, _):
        s = against(0, qb[pl.ds(2 * i, 2)].reshape(2 * T, H)) * SCALE
        for n in range(2):
            o = 2 * i + n
            lanes = slice(n * T, (n + 1) * T)
            position = dev(x, o, c) * T + lax.broadcasted_iota(jnp.int32, (1, T), 1)
            same = ckb[...].reshape(KEYS, T) == cq[o][0:1, :]
            allowed = same & (pkb[...].reshape(KEYS, T) <= position)
            masked = jnp.where(allowed, s[:, lanes], NEG)
            top = jnp.max(masked, axis=0, keepdims=True)
            e = jnp.where(allowed, jnp.exp(masked - top), 0.0)
            eb[o] = e
            eh[i, :, lanes], el[i, :, lanes] = split(e)
            mlb[y, 0, pl.ds(o, 1), :] = top
            mlb[y, 1, pl.ds(o, 1), :] = jnp.sum(e, axis=0, keepdims=True)
        return 0

    lax.fori_loop(0, Y // 2, scores, 0)
    far_y = (4, 3, 5, 2, 6, 1, 7)
    ml_in, r_in = Batch(), Batch()
    for d in far_y:
        ml_in.share(mlb.at[y], dev(x, yy(d), c))
    v_own.wait_recv()
    sides(1, x, 1 - c)
    v_sib = collect(1, v_x)
    for d, copy in v_sib:
        copy.wait_recv()
        sides(1, xx(-d), 1 - c)
    tree_g.finish()

    def products(i, _):
        gv = against(1, gb[pl.ds(2 * i, 2)].reshape(2 * T, H))
        for n in range(2):
            o = 2 * i + n
            gvn = gv[:, n * T:(n + 1) * T]
            gvb[o] = gvn
            rb[y, pl.ds(o, 1), :] = jnp.sum(eb[o] * gvn, axis=0, keepdims=True)
        return 0

    lax.fori_loop(0, Y // 2, products, 0)
    for d in far_y:
        r_in.share(rb.at[y], dev(x, yy(d), c))

    ml_in.wait_recv()
    top = mlb[0, 0]
    for o in range(1, Y):
        top = jnp.maximum(top, mlb[o, 0])
    factors = [jnp.exp(mlb[o, 0] - top) for o in range(Y)]
    total = mlb[0, 1] * factors[0]
    for o in range(1, Y):
        total = total + mlb[o, 1] * factors[o]
    al_s[...] = jnp.exp(mlb[y, 0] - top) / total

    def scaled(i, _):
        for n in range(2):
            o = 2 * i + n
            rows = slice(n * T, (n + 1) * T)
            column = jnp.transpose(jnp.broadcast_to(al_s[pl.ds(o, 1), :], (T, T)))
            gsc[i, rows, 0:H], gsc[i, rows, H:] = split(gb[o] * column)
            qsc[i, rows, 0:H], qsc[i, rows, H:] = split(qb[o] * (column * SCALE))
        return 0

    lax.fori_loop(0, Y // 2, scaled, 0)

    def query_side(n, hi, lo, into, factor):
        def body(i, _):
            both = jnp.dot(kvt[n], hi[i], preferred_element_type=F32)
            r = both[0:H] + both[H:] + jnp.dot(kvt[n, 0:H], lo[i], preferred_element_type=F32)
            for m in range(2):
                o = 2 * i + m
                into[o] = r[:, m * T:(m + 1) * T] * (al_s[pl.ds(o, 1), :] * factor)
            return 0

        lax.fori_loop(0, Y // 2, body, 0)

    def key_side(n, d, hi, lo, with_):
        xo = xx(d)
        rows = pl.ds(pl.multiple_of(xo * (C * T), C * T), C * T)

        def add(i, acc):
            both = jnp.dot(hi[i, rows, :], with_[i], preferred_element_type=F32)
            rest = jnp.dot(lo[i, rows, :], with_[i, :, 0:H], preferred_element_type=F32)
            return acc + (both[:, 0:H] + both[:, H:] + rest)

        acc = lax.fori_loop(0, Y // 2, add, jnp.zeros((C * T, H), F32))
        gkv[n, xo] = acc.reshape(C, T, H)
        return start(gkv.at[n, xo, 1 - c], gsib.at[n, xo], sib)

    x_in = Batch()

    def key_send(n, d, copy):
        copy.wait_recv()
        gkv[n, xx(d), c] += gsib[n, xx(d)]
        if d:
            x_in.start(gkv.at[n, xx(d), c], gx.at[d - 1, n], dev(xx(d), y, c))

    query_side(1, eh, el, ob, 1.0)
    ring_o = Scatter(
        lambda o: ob.at[o], lambda o, h: ob.at[o, pl.ds(64 * h, 64)],
        lambda h, k: (obr, obl)[h].at[k], (obr.at[0, pl.ds(0, 64)], obl.at[0, pl.ds(64, 64)]),
    )
    far_x = (2, 1, 3, 0)
    last = None
    for d in far_x:
        copy = key_side(1, d, eh, el, gsc)
        if last is not None:
            key_send(1, *last)
        last = (d, copy)
    key_send(1, *last)
    ring_o.step(1)

    r_in.wait_recv()
    row = rb[0] * factors[0]
    for o in range(1, Y):
        row = row + rb[o] * factors[o]
    rr_s[...] = row / total

    def slopes(i, _):
        for n in range(2):
            o = 2 * i + n
            lanes = slice(n * T, (n + 1) * T)
            dh[i, :, lanes], dl[i, :, lanes] = split(eb[o] * (gvb[o] - rr_s[pl.ds(o, 1), :]))
        return 0

    lax.fori_loop(0, Y // 2, slopes, 0)

    last = (2, key_side(0, 2, dh, dl, qsc))
    query_side(0, dh, dl, gqb, SCALE)
    sum_q = Sum(
        lambda o: [gqb.at[o]], lambda o, h: [gqb.at[o, pl.ds(64 * h, 64)]],
        lambda h, k: [gq_in.at[h, k]], lambda h: [gq_half.at[h]],
    )
    sum_q.near()
    for d in far_x[1:]:
        copy = key_side(0, d, dh, dl, qsc)
        key_send(0, *last)
        last = (d, copy)
    sum_q.step()
    ring_o.step(2)
    key_send(0, *last)
    sum_q.finish()
    ring_o.step(3)
    x_in.wait_recv()
    parts = [jnp.transpose(gqb[y])]
    for n in range(2):
        parts.append((gkv[n, x, c] + gx[0, n]) + (gx[1, n] + gx[2, n]))
    grads = split(jnp.concatenate(parts, axis=1))

    y_order = (4, 3, -3, 2, -2, 1, -1, 0)

    def project(d):
        xo = xx(d)
        rows = pl.ds(pl.multiple_of(xo * (D // X), D // X), D // X)
        gw[xo] = dot3((toth[rows, :], totl[rows, :]), grads, NN).reshape(Y, C, 2, 16, 3 * H)
        return start(gw.at[xo, :, 1 - c], gws.at[xo], sib)

    def sum_for(*ds):
        return Sum(
            lambda o: [gw.at[xx(d), o, c, 0] for d in ds],
            lambda o, h: [gw.at[xx(d), o, c, 0, pl.ds(8 * h, 8)] for d in ds],
            lambda h, k: [(ga_r, ga_l)[h].at[d, k] for d in ds],
            lambda h: [(ga_r, ga_l)[h].at[d, 3, pl.ds(0, 8)] for d in ds],
        )

    bx_in = {n: Batch() for n in y_order}

    def launch(d, copy):
        copy.wait_recv()
        xo = xx(d)
        gw[xo, :, c] += gws[xo]
        if d:
            for n in y_order:
                o = yy(n)
                bx_in[n].start(gw.at[xo, o, c, 1], gbx.at[d - 1, o], dev(xo, y, c))

    first, second, third, fourth = [(d, project(d)) for d in far_x]
    launch(*first)
    launch(*second)
    sum_a = [sum_for(first[0], second[0])]
    launch(*third)
    launch(*fourth)
    sum_a.append(sum_for(third[0], fourth[0]))
    for tree in sum_a:
        tree.near()

    def gathered(*numbers):
        for n in numbers:
            o = yy(n)
            bx_in[n].wait_recv()
            gw[x, o, c, 1] += (gbx[0, o] + gbx[1, o]) + gbx[2, o]

    sum_a[0].step()
    gathered(4, 3, -3)
    sum_b = Sum(
        lambda o: [gw.at[x, o, c, 1]], lambda o, h: [gw.at[x, o, c, 1, pl.ds(8 * h, 8)]],
        lambda h, k: [(gb_r, gb_l)[h].at[k]], lambda h: [(gb_r, gb_l)[h].at[3, pl.ds(0, 8)]],
    )
    sum_a[1].step()
    gathered(2, -2)
    gathered(1, -1)
    sum_b.near()
    sum_b.step()
    gathered(0)
    a_in = Batch()
    for tree, pair in zip(sum_a, (far_x[:2], far_x[2:])):
        tree.finish()
        for d in pair:
            if d:
                a_in.start(gw.at[xx(d), y, c, 0], gax.at[d - 1], dev(xx(d), y, c))
    sum_b.finish()
    ring_o.step(4)
    att_o[...] = jnp.transpose(ob[y])
    grad_o[16:32, :] = gw[x, y, c, 1]
    a_in.wait_recv()
    grad_o[0:16, :] = (gw[x, y, c, 0] + gax[0]) + (gax[1] + gax[2])
    for i, rows in enumerate(sends):
        some = sizer.at[pl.ds(0, rows)]
        pltpu.make_async_copy(some, some, send.at[i]).wait()


def results(att, grad, att_o, gq_o, gk_o, gv_o):
    att_o[...] = att[...]
    for i, ref in enumerate((gq_o, gk_o, gv_o)):
        ref[...] = grad[:, i * H:(i + 1) * H]


def local(tokens, cluster, w_query, w_key, w_value, grad_out):
    vmem = pl.BlockSpec(memory_space=pltpu.VMEM)
    hbm = pl.BlockSpec(memory_space=pl.ANY)
    W3 = 3 * H
    keys = X * C * T
    pairs = Y // 2
    scratch = [
        pltpu.VMEM((T, D), F32),
        pltpu.VMEM((X, Y, C, 2, 16, W3), F32),
        pltpu.VMEM((T, D), BF16), pltpu.VMEM((T, D), BF16),
        pltpu.VMEM((D, T), BF16), pltpu.VMEM((D, T), BF16),
        pltpu.VMEM((Y, T, H), F32), pltpu.VMEM((Y, T, H), F32),
        pltpu.VMEM((2, X, C, T, H), F32),
        pltpu.VMEM((Y, 8, T), F32), pltpu.VMEM((X, C, 8, T), F32),
        pltpu.VMEM((X * C, T, T), F32), pltpu.VMEM((X * C, T, T), jnp.int32),
        pltpu.VMEM((2, keys, 2 * H), BF16), pltpu.VMEM((2, 2 * H, keys), BF16),
        pltpu.VMEM((pairs, 2 * T, 2 * H), BF16), pltpu.VMEM((pairs, 2 * T, 2 * H), BF16),
        pltpu.VMEM((Y, keys, T), F32), pltpu.VMEM((Y, keys, T), F32),
        pltpu.VMEM((pairs, keys, 2 * T), BF16), pltpu.VMEM((pairs, keys, 2 * T), BF16),
        pltpu.VMEM((pairs, keys, 2 * T), BF16), pltpu.VMEM((pairs, keys, 2 * T), BF16),
        pltpu.VMEM((Y, 2, Y, T), F32), pltpu.VMEM((Y, Y, T), F32),
        pltpu.VMEM((Y, T), F32), pltpu.VMEM((Y, T), F32),
        pltpu.VMEM((Y, H, T), F32),
        pltpu.VMEM((4, H, T), F32), pltpu.VMEM((4, H, T), F32),
        pltpu.VMEM((Y, H, T), F32),
        pltpu.VMEM((2, 3, H, T), F32), pltpu.VMEM((2, H // 2, T), F32),
        pltpu.VMEM((2, X, C, T, H), F32),
        pltpu.VMEM((2, X, T, H), F32),
        pltpu.VMEM((X - 1, 2, T, H), F32),
        pltpu.VMEM((X, Y, C, 2, 16, W3), F32),
        pltpu.VMEM((X, Y, 2, 16, W3), F32),
        pltpu.VMEM((X, 4, 16, W3), F32), pltpu.VMEM((X, 4, 16, W3), F32),
        pltpu.VMEM((X - 1, Y, 16, W3), F32),
        pltpu.VMEM((4, 16, W3), F32), pltpu.VMEM((4, 16, W3), F32),
        pltpu.VMEM((X - 1, 16, W3), F32),
        pltpu.VMEM((ROWS, 128), F32),
        pltpu.SemaphoreType.DMA((4,)),
        pltpu.SemaphoreType.DMA((COPIES,)),
        pltpu.SemaphoreType.DMA((8,)),
    ]
    att, grad = pl.pallas_call(
        kernel,
        out_shape=(
            jax.ShapeDtypeStruct((T, H), F32),
            jax.ShapeDtypeStruct((D // 64, W3), F32),
        ),
        in_specs=[hbm, vmem, hbm, hbm, hbm, hbm],
        out_specs=(vmem,) * 2,
        scratch_shapes=scratch,
        compiler_params=pltpu.CompilerParams(
            collective_id=0, has_side_effects=True, vmem_limit_bytes=58 * 1024 * 1024
        ),
        name="routing",
    )(tokens, cluster.reshape(1, T), w_query, w_key, w_value, grad_out)
    part = jax.ShapeDtypeStruct((D // 64, H), F32)
    return pl.pallas_call(
        results,
        out_shape=(jax.ShapeDtypeStruct((T, H), F32), part, part, part),
        in_specs=[vmem] * 2,
        out_specs=(vmem,) * 4,
        name="results",
    )(att, grad)


def solution(mesh):
    in_specs = (P("seq", None), P("seq", None)) + (P("seq", "head"),) * 4
    out_specs = (P("seq", "head"),) * 4
    return jax.shard_map(local, mesh=mesh, in_specs=in_specs, out_specs=out_specs, check_vma=False)
```

time: 104 us -> 95.9 us (0.922)
  Pallas kernels: 103 us -> 95 us
    pallas_call x1, Pallas kernels: 101 us -> 93.5 us  [local(): pl.pallas_call(kernel, out_shape=(jax.ShapeDtypeStruct((T, H), F32), jax....]
where the time goes in v2:
time: 95.9 us; the launch traced here: 95.6 us
  Pallas kernels  95 us (99%)
    pallas_call x1, Pallas kernels, local(): pl.pallas_call(kernel, out_shape=(jax.ShapeDtypeStruct((T, H), F32), jax....  93.5 us

profile of v2, /device:TPU:6, one launch (start us, length us, event | category | flops | bytes accessed | tf_op | source)
XLA Modules:
  0.0 95.6 jit_solution(13062587452599975343)
XLA Ops:
  0.6 93.5 %routing.1 = (f32[128,128]{1,0:T(8,128)}, f32[32,384]{1,0:T(8,128)}) custom-call(f32[128,2048]{1,0:T(8,128)} %tok_in.1, s32[1,128]{1,0:T(1,128)} %bitcast.1, f32[32,128]{1,0:T(8,128)} %wq.1, f32[32,128]{1,0:T(8,128)} %wk.1, f32[32,128]{1,0:T(8,128)} %wv.1, f32[128,128]{1,0:T(8,128)} %gout.1), custom_call_target="tpu_custom_call" | custom-call | tf_op jit(solution)/shard_map/routing/pallas_call | solution.py:604
  94.2 1.5 %results.1 = (f32[128,128]{1,0:T(8,128)}, f32[32,128]{1,0:T(8,128)}, f32[32,128]{1,0:T(8,128)}, f32[32,128]{1,0:T(8,128)}) custom-call(f32[128,128]{1,0:T(8,128)} %get-tuple-element.6.att, f32[32,384]{1,0:T(8,128)} %get-tuple-element.7.grad), custom_call_target="tpu_custom_call" | custom-call | tf_op jit(solution)/shard_map/results/pallas_call | solution.py:619

commit v3 on v2

--- a/solution.py
+++ b/solution.py
@@ -17,7 +17,7 @@
 D = 2048
 SCALE = 1.0 / math.sqrt(H)
 NEG = -1e30
-COPIES = 136
+COPIES = 168
 ROWS = 8192
 
 NT = ((1,), (1,))
@@ -42,6 +42,7 @@
     tok, wbuf, tokh, tokl, toth, totl, qb, gb, kv, cq, ck, ckb, pkb,
     kvc, kvt, qsc, gsc, eb, gvb, eh, el, dh, dl, mlb, rb, al_s, rr_s,
     ob, obr, obl, gqb, gq_in, gq_half, gkv, gsib, gx, gw, gws, ga_r, ga_l, gbx, gb_r, gb_l, gax,
+    vw, vws, va_r, va_l, vbx, vb_r, vb_l, vax,
     sizer, send, recv, here,
 ):
     me = lax.axis_index("seq")
@@ -302,7 +303,6 @@
     sides(1, x, c)
     k_own.wait_recv()
     sides(0, x, 1 - c)
-    tree_g.step()
     tree_q.step()
     ids_in.wait_recv()
 
@@ -322,13 +322,19 @@
             sides(n, xx(-d), c)
         return over
 
+    tree_g.step()
     k_sib = collect(0, k_x)
     for d, copy in k_sib:
         copy.wait_recv()
         sides(0, xx(-d), 1 - c)
-    tree_q.finish()
 
     KEYS = X * C * T
+
+    def pair(j):
+        return lax.rem(y // 2 + j * (2 * lax.rem(y, 2) - 1) + 12, Y // 2)
+
+    def pairs(body, first, last):
+        lax.fori_loop(first, last, lambda j, carry: body(pair(j), carry), 0)
 
     def against(n, rows):
         hi, lo = split(rows)
@@ -352,7 +358,9 @@
             mlb[y, 1, pl.ds(o, 1), :] = jnp.sum(e, axis=0, keepdims=True)
         return 0
 
-    lax.fori_loop(0, Y // 2, scores, 0)
+    pairs(scores, 0, 2)
+    tree_q.finish()
+    pairs(scores, 2, 4)
     far_y = (4, 3, 5, 2, 6, 1, 7)
     ml_in, r_in = Batch(), Batch()
     for d in far_y:
@@ -363,7 +371,6 @@
     for d, copy in v_sib:
         copy.wait_recv()
         sides(1, xx(-d), 1 - c)
-    tree_g.finish()
 
     def products(i, _):
         gv = against(1, gb[pl.ds(2 * i, 2)].reshape(2 * T, H))
@@ -374,7 +381,9 @@
             rb[y, pl.ds(o, 1), :] = jnp.sum(eb[o] * gvn, axis=0, keepdims=True)
         return 0
 
-    lax.fori_loop(0, Y // 2, products, 0)
+    pairs(products, 0, 2)
+    tree_g.finish()
+    pairs(products, 2, 4)
     for d in far_y:
         r_in.share(rb.at[y], dev(x, yy(d), c))
 
@@ -399,7 +408,7 @@
 
     lax.fori_loop(0, Y // 2, scaled, 0)
 
-    def query_side(n, hi, lo, into, factor):
+    def query_side(n, hi, lo, into, factor, first, last):
         def body(i, _):
             both = jnp.dot(kvt[n], hi[i], preferred_element_type=F32)
             r = both[0:H] + both[H:] + jnp.dot(kvt[n, 0:H], lo[i], preferred_element_type=F32)
@@ -408,7 +417,7 @@
                 into[o] = r[:, m * T:(m + 1) * T] * (al_s[pl.ds(o, 1), :] * factor)
             return 0
 
-        lax.fori_loop(0, Y // 2, body, 0)
+        pairs(body, first, last)
 
     def key_side(n, d, hi, lo, with_):
         xo = xx(d)
@@ -423,19 +432,14 @@
         gkv[n, xo] = acc.reshape(C, T, H)
         return start(gkv.at[n, xo, 1 - c], gsib.at[n, xo], sib)
 
-    x_in = Batch()
+    x_in = [Batch(), Batch()]
 
     def key_send(n, d, copy):
         copy.wait_recv()
         gkv[n, xx(d), c] += gsib[n, xx(d)]
         if d:
-            x_in.start(gkv.at[n, xx(d), c], gx.at[d - 1, n], dev(xx(d), y, c))
-
-    query_side(1, eh, el, ob, 1.0)
-    ring_o = Scatter(
-        lambda o: ob.at[o], lambda o, h: ob.at[o, pl.ds(64 * h, 64)],
-        lambda h, k: (obr, obl)[h].at[k], (obr.at[0, pl.ds(0, 64)], obl.at[0, pl.ds(64, 64)]),
-    )
+            x_in[n].start(gkv.at[n, xx(d), c], gx.at[d - 1, n], dev(xx(d), y, c))
+
     far_x = (2, 1, 3, 0)
     last = None
     for d in far_x:
@@ -444,7 +448,6 @@
             key_send(1, *last)
         last = (d, copy)
     key_send(1, *last)
-    ring_o.step(1)
 
     r_in.wait_recv()
     row = rb[0] * factors[0]
@@ -461,95 +464,135 @@
 
     lax.fori_loop(0, Y // 2, slopes, 0)
 
+    y_order = (4, 3, -3, 2, -2, 1, -1, 0)
+
+    class Weight:
+        def __init__(self, buf, from_sib, a_r, a_l, bx, b_r, b_l, ax):
+            self.buf, self.from_sib, self.a, self.bx = buf, from_sib, (a_r, a_l), bx
+            self.b, self.ax = (b_r, b_l), ax
+            self.width = buf.shape[-1]
+
+        def project(self, d, grads):
+            xo = xx(d)
+            rows = pl.ds(pl.multiple_of(xo * (D // X), D // X), D // X)
+            part = dot3((toth[rows, :], totl[rows, :]), grads, NN)
+            self.buf[xo] = part.reshape(Y, C, 2, 16, self.width)
+            return d, start(self.buf.at[xo, :, 1 - c], self.from_sib.at[xo], sib)
+
+        def launch(self, d, copy):
+            copy.wait_recv()
+            xo = xx(d)
+            self.buf[xo, :, c] += self.from_sib[xo]
+            if d:
+                for n in y_order:
+                    o = yy(n)
+                    self.bx_in[n].start(self.buf.at[xo, o, c, 1], self.bx.at[d - 1, o], dev(xo, y, c))
+
+        def sum_for(self, *ds):
+            return Sum(
+                lambda o: [self.buf.at[xx(d), o, c, 0] for d in ds],
+                lambda o, h: [self.buf.at[xx(d), o, c, 0, pl.ds(8 * h, 8)] for d in ds],
+                lambda h, k: [self.a[h].at[d, k] for d in ds],
+                lambda h: [self.a[h].at[d, 3, pl.ds(0, 8)] for d in ds],
+            )
+
+        def begin(self, grads):
+            self.bx_in = {n: Batch() for n in y_order}
+            made = [self.project(d, grads) for d in far_x]
+            self.launch(*made[0])
+            self.launch(*made[1])
+            self.sum_a = [self.sum_for(*far_x[:2])]
+            self.launch(*made[2])
+            self.launch(*made[3])
+            self.sum_a.append(self.sum_for(*far_x[2:]))
+            for tree in self.sum_a:
+                tree.near()
+
+        def gathered(self, *numbers):
+            for n in numbers:
+                o = yy(n)
+                self.bx_in[n].wait_recv()
+                self.buf[x, o, c, 1] += (self.bx[0, o] + self.bx[1, o]) + self.bx[2, o]
+
+        def first(self):
+            self.sum_a[0].step()
+            self.gathered(4, 3, -3)
+            self.sum_b = Sum(
+                lambda o: [self.buf.at[x, o, c, 1]], lambda o, h: [self.buf.at[x, o, c, 1, pl.ds(8 * h, 8)]],
+                lambda h, k: [self.b[h].at[k]], lambda h: [self.b[h].at[3, pl.ds(0, 8)]],
+            )
+
+        def second(self):
+            self.sum_a[1].step()
+            self.gathered(2, -2, 1, -1)
+            self.sum_b.near()
+
+        def third(self):
+            self.sum_b.step()
+            self.gathered(0)
+
+        def late(self):
+            self.a_in = Batch()
+            for tree, pair in zip(self.sum_a, (far_x[:2], far_x[2:])):
+                tree.finish()
+                for d in pair:
+                    if d:
+                        self.a_in.start(self.buf.at[xx(d), y, c, 0], self.ax.at[d - 1], dev(xx(d), y, c))
+            self.sum_b.finish()
+
+        def result(self, lanes):
+            grad_o[16:32, lanes] = self.buf[x, y, c, 1]
+            self.a_in.wait_recv()
+            ax = self.ax
+            grad_o[0:16, lanes] = (self.buf[x, y, c, 0] + ax[0]) + (ax[1] + ax[2])
+
+    def key_total(n):
+        x_in[n].wait_recv()
+        return (gkv[n, x, c] + gx[0, n]) + (gx[1, n] + gx[2, n])
+
+    w_qk = Weight(gw, gws, ga_r, ga_l, gbx, gb_r, gb_l, gax)
+    w_v = Weight(vw, vws, va_r, va_l, vbx, vb_r, vb_l, vax)
+
     last = (2, key_side(0, 2, dh, dl, qsc))
-    query_side(0, dh, dl, gqb, SCALE)
+    query_side(0, dh, dl, gqb, SCALE, 2, 4)
     sum_q = Sum(
         lambda o: [gqb.at[o]], lambda o, h: [gqb.at[o, pl.ds(64 * h, 64)]],
         lambda h, k: [gq_in.at[h, k]], lambda h: [gq_half.at[h]],
     )
+    query_side(0, dh, dl, gqb, SCALE, 0, 2)
     sum_q.near()
-    for d in far_x[1:]:
+    w_v.begin(split(key_total(1)))
+    copy = key_side(0, far_x[1], dh, dl, qsc)
+    key_send(0, *last)
+    last = (far_x[1], copy)
+    for d in far_x[2:]:
         copy = key_side(0, d, dh, dl, qsc)
         key_send(0, *last)
         last = (d, copy)
+    key_send(0, *last)
     sum_q.step()
+    query_side(1, eh, el, ob, 1.0, 0, 4)
+    ring_o = Scatter(
+        lambda o: ob.at[o], lambda o, h: ob.at[o, pl.ds(64 * h, 64)],
+        lambda h, k: (obr, obl)[h].at[k], (obr.at[0, pl.ds(0, 64)], obl.at[0, pl.ds(64, 64)]),
+    )
+    w_v.first()
+    w_v.second()
+    sum_q.finish()
+    ring_o.step(1)
+    w_qk.begin(split(jnp.concatenate([jnp.transpose(gqb[y]), key_total(0)], axis=1)))
+    w_v.third()
     ring_o.step(2)
-    key_send(0, *last)
-    sum_q.finish()
+    w_qk.first()
+    w_v.late()
+    w_qk.second()
     ring_o.step(3)
-    x_in.wait_recv()
-    parts = [jnp.transpose(gqb[y])]
-    for n in range(2):
-        parts.append((gkv[n, x, c] + gx[0, n]) + (gx[1, n] + gx[2, n]))
-    grads = split(jnp.concatenate(parts, axis=1))
-
-    y_order = (4, 3, -3, 2, -2, 1, -1, 0)
-
-    def project(d):
-        xo = xx(d)
-        rows = pl.ds(pl.multiple_of(xo * (D // X), D // X), D // X)
-        gw[xo] = dot3((toth[rows, :], totl[rows, :]), grads, NN).reshape(Y, C, 2, 16, 3 * H)
-        return start(gw.at[xo, :, 1 - c], gws.at[xo], sib)
-
-    def sum_for(*ds):
-        return Sum(
-            lambda o: [gw.at[xx(d), o, c, 0] for d in ds],
-            lambda o, h: [gw.at[xx(d), o, c, 0, pl.ds(8 * h, 8)] for d in ds],
-            lambda h, k: [(ga_r, ga_l)[h].at[d, k] for d in ds],
-            lambda h: [(ga_r, ga_l)[h].at[d, 3, pl.ds(0, 8)] for d in ds],
-        )
-
-    bx_in = {n: Batch() for n in y_order}
-
-    def launch(d, copy):
-        copy.wait_recv()
-        xo = xx(d)
-        gw[xo, :, c] += gws[xo]
-        if d:
-            for n in y_order:
-                o = yy(n)
-                bx_in[n].start(gw.at[xo, o, c, 1], gbx.at[d - 1, o], dev(xo, y, c))
-
-    first, second, third, fourth = [(d, project(d)) for d in far_x]
-    launch(*first)
-    launch(*second)
-    sum_a = [sum_for(first[0], second[0])]
-    launch(*third)
-    launch(*fourth)
-    sum_a.append(sum_for(third[0], fourth[0]))
-    for tree in sum_a:
-        tree.near()
-
-    def gathered(*numbers):
-        for n in numbers:
-            o = yy(n)
-            bx_in[n].wait_recv()
-            gw[x, o, c, 1] += (gbx[0, o] + gbx[1, o]) + gbx[2, o]
-
-    sum_a[0].step()
-    gathered(4, 3, -3)
-    sum_b = Sum(
-        lambda o: [gw.at[x, o, c, 1]], lambda o, h: [gw.at[x, o, c, 1, pl.ds(8 * h, 8)]],
-        lambda h, k: [(gb_r, gb_l)[h].at[k]], lambda h: [(gb_r, gb_l)[h].at[3, pl.ds(0, 8)]],
-    )
-    sum_a[1].step()
-    gathered(2, -2)
-    gathered(1, -1)
-    sum_b.near()
-    sum_b.step()
-    gathered(0)
-    a_in = Batch()
-    for tree, pair in zip(sum_a, (far_x[:2], far_x[2:])):
-        tree.finish()
-        for d in pair:
-            if d:
-                a_in.start(gw.at[xx(d), y, c, 0], gax.at[d - 1], dev(xx(d), y, c))
-    sum_b.finish()
+    w_qk.third()
+    w_qk.late()
+    w_v.result(slice(2 * H, 3 * H))
+    w_qk.result(slice(0, 2 * H))
     ring_o.step(4)
     att_o[...] = jnp.transpose(ob[y])
-    grad_o[16:32, :] = gw[x, y, c, 1]
-    a_in.wait_recv()
-    grad_o[0:16, :] = (gw[x, y, c, 0] + gax[0]) + (gax[1] + gax[2])
     for i, rows in enumerate(sends):
         some = sizer.at[pl.ds(0, rows)]
         pltpu.make_async_copy(some, some, send.at[i]).wait()
@@ -567,6 +610,7 @@
     W3 = 3 * H
     keys = X * C * T
     pairs = Y // 2
+    sums = []
     scratch = [
         pltpu.VMEM((T, D), F32),
         pltpu.VMEM((X, Y, C, 2, 16, W3), F32),
@@ -590,17 +634,19 @@
         pltpu.VMEM((2, X, C, T, H), F32),
         pltpu.VMEM((2, X, T, H), F32),
         pltpu.VMEM((X - 1, 2, T, H), F32),
-        pltpu.VMEM((X, Y, C, 2, 16, W3), F32),
-        pltpu.VMEM((X, Y, 2, 16, W3), F32),
-        pltpu.VMEM((X, 4, 16, W3), F32), pltpu.VMEM((X, 4, 16, W3), F32),
-        pltpu.VMEM((X - 1, Y, 16, W3), F32),
-        pltpu.VMEM((4, 16, W3), F32), pltpu.VMEM((4, 16, W3), F32),
-        pltpu.VMEM((X - 1, 16, W3), F32),
         pltpu.VMEM((ROWS, 128), F32),
         pltpu.SemaphoreType.DMA((4,)),
         pltpu.SemaphoreType.DMA((COPIES,)),
         pltpu.SemaphoreType.DMA((8,)),
     ]
+    for wide in (2 * H, H):
+        ring = pltpu.VMEM((X, 4, 16, wide), F32)
+        small = pltpu.VMEM((4, 16, wide), F32)
+        sums += [
+            pltpu.VMEM((X, Y, C, 2, 16, wide), F32), pltpu.VMEM((X, Y, 2, 16, wide), F32), ring, ring,
+            pltpu.VMEM((X - 1, Y, 16, wide), F32), small, small, pltpu.VMEM((X - 1, 16, wide), F32),
+        ]
+    scratch[-4:-4] = sums
     att, grad = pl.pallas_call(
         kernel,
         out_shape=(

time: 95.9 us -> 93.1 us (0.971)
  Pallas kernels: 95 us -> 92.2 us
    pallas_call x1, Pallas kernels: 93.5 us -> 90.7 us  [local(): pl.pallas_call(kernel, out_shape=(jax.ShapeDtypeStruct((T, H), F32), jax....]
where the time goes in v3:
time: 93.1 us; the launch traced here: 92.9 us
  Pallas kernels  92.2 us (99%)
    pallas_call x1, Pallas kernels, local(): pl.pallas_call(kernel, out_shape=(jax.ShapeDtypeStruct((T, H), F32), jax....  90.7 us

profile of v3, /device:TPU:6, one launch (start us, length us, event | category | flops | bytes accessed | tf_op | source)
XLA Modules:
  0.0 92.9 jit_solution(2895254733885426545)
XLA Ops:
  0.6 90.7 %routing.1 = (f32[128,128]{1,0:T(8,128)}, f32[32,384]{1,0:T(8,128)}) custom-call(f32[128,2048]{1,0:T(8,128)} %tok_in.1, s32[1,128]{1,0:T(1,128)} %bitcast.1, f32[32,128]{1,0:T(8,128)} %wq.1, f32[32,128]{1,0:T(8,128)} %wk.1, f32[32,128]{1,0:T(8,128)} %wv.1, f32[128,128]{1,0:T(8,128)} %gout.1), custom_call_target="tpu_custom_call" | custom-call | tf_op jit(solution)/shard_map/routing/pallas_call | solution.py:650
  91.4 1.5 %results.1 = (f32[128,128]{1,0:T(8,128)}, f32[32,128]{1,0:T(8,128)}, f32[32,128]{1,0:T(8,128)}, f32[32,128]{1,0:T(8,128)}) custom-call(f32[128,128]{1,0:T(8,128)} %get-tuple-element.6.att, f32[32,384]{1,0:T(8,128)} %get-tuple-element.7.grad), custom_call_target="tpu_custom_call" | custom-call | tf_op jit(solution)/shard_map/results/pallas_call | solution.py:665
